TPU v7x, 512 devices: a whole 4x8x8 slice. The times are simulated.
512 devices in a mesh: row: 256 (over z, y, x), col: 2 (over core).
Axes of the slice: x: 4, y: 8, z: 8, core: 2. Of those that a mesh axis runs over, the one named last changes fastest.
Arguments:
- panel: bfloat16 [262144, 4096], P('row', 'col'), may hold values from -60 to 60, as said below
- sketch: bfloat16 [4096, 256], P('col'), may hold values from -0.09375 to 0.09375
Outputs:
- basis: float32 [262144, 256], P(('row', 'col'))
- upper: float32 [256, 256], replicated
Inputs may be any that keep to these rules, and one draw needn't show every extreme that they name: `panel`: scaled expression values, real-valued, with scales that differ from cell to cell and from gene to gene.
All inputs are finite; a program needn't handle non-finite values.
Results may differ from a plain program's by a relative error of at most 0.0003.
Values sent between devices are 32-bit elements; how exact they have to be, the bound alone decides.
No kernel may reach another device: no remote copies, remote signals or barrier semaphores. Data moves between devices by JAX's collectives and lax.ppermute only.
A program may use at most 64 MiB of HBM per device.

v0:
```python
import jax
import jax.numpy as jnp
from jax import lax
from jax.sharding import Mesh
from jax.sharding import PartitionSpec as P

ROW = ("row_0", "row_1", "row_2")
ROW_COL = ("row_0", "row_1", "row_2", "col")


def from_everyone(x, axis):
    size = lax.axis_size(axis)
    return lax.all_to_all(jnp.broadcast_to(x[None], (size, *x.shape)), axis, 0, 0, tiled=True)


def taken_together(x, axis):
    everything = from_everyone(x, axis)
    return jnp.sum(everything, axis=0)


def padded_to(lines, size):
    spare = -lines.shape[0] % size
    if not spare:
        return lines
    return jnp.concatenate([lines, jnp.zeros((spare, *lines.shape[1:]), lines.dtype)])


def laid_out(blocks, dim):
    blocks = jnp.moveaxis(blocks, 0, dim)
    dims = blocks.shape
    return blocks.reshape(*dims[:dim], dims[dim] * dims[dim + 1], *dims[dim + 2 :])


def whole_of(x, axes, dim):
    far, near = axes
    initial = from_everyone(x, far)
    blocks = jnp.swapaxes(from_everyone(initial, near), 0, 1)
    return laid_out(blocks.reshape(-1, *x.shape), dim)


def split_up(x, dim, size):
    before, after = (x.shape[:dim], x.shape[dim + 1 :])
    return jnp.moveaxis(x.reshape(*before, size, -1, *after), dim, 0)


def sum_at_owner(x, axis, dim):
    blocks = split_up(x, dim, lax.axis_size(axis))
    arrived = lax.all_to_all(blocks, axis, split_axis=0, concat_axis=0, tiled=True)
    return arrived.sum(axis=0)


def sum_by_axis(x, axes, dim):
    far, near = axes
    blocks = split_up(x, dim, lax.axis_size(far))
    nearer = sum_at_owner(blocks, near, dim + 1)
    arrived = lax.all_to_all(nearer, far, split_axis=0, concat_axis=0, tiled=True)
    return arrived.sum(axis=0)


def nested_sum(x, axes):
    lines = x.reshape(-1, x.shape[-1])
    padded = padded_to(lines, lax.axis_size(axes[0]) * lax.axis_size(axes[1]))
    whole = whole_of(sum_by_axis(padded, axes, 0), axes, 0)
    return lax.slice_in_dim(whole, 0, len(lines)).reshape(x.shape)


def local(panel, sketch):
    rows = panel.shape[0]
    share = rows // lax.axis_size("col")
    total_rows = rows * lax.axis_size(ROW)
    partial_value = jnp.dot(panel, sketch, preferred_element_type=jnp.float32)
    whole = taken_together(partial_value, "col")
    local_gram = jnp.dot(whole.T, whole, precision=lax.Precision.HIGHEST)
    gram = nested_sum(local_gram, (("row_0", "row_1"), "row_2")) / total_rows
    offset = lax.axis_index("col") * share
    block = lax.dynamic_slice_in_dim(whole, offset, share, 0)
    factor = jnp.linalg.cholesky(gram).T
    basis = jax.scipy.linalg.solve_triangular(factor.T, block.T, lower=True).T
    return (basis, factor)


def solution(mesh):
    finer = Mesh(
        mesh.devices.reshape(8, 8, 4, mesh.shape["col"]), ("row_0", "row_1", "row_2", "col")
    )
    in_specs = (P(ROW, "col"), P("col", None))
    out_specs = (P(ROW_COL, None), P())
    return jax.shard_map(local, mesh=finer, in_specs=in_specs, out_specs=out_specs, check_vma=False)
```

profile of v0, /device:TPU:8, one launch (start us, length us, event | category | flops | bytes accessed | tf_op | source)
XLA Modules:
  0.0 149.0 jit_solution(4076398592736521429)
XLA Ops:
  0.6 1.2 copy-done
  1.9 3.4 %fusion.13 = f32[1024,256]{1,0:T(8,128)S(1)} fusion(bf16[1024,2048]{1,0:T(8,128)(2,1)} %param.2, bf16[2048,256]{1,0:T(8,128)(2,1)S(1)} %copy-done), kind=kOutput, calls=%fused_computation.37 | convolution fusion | flops 1073741824 | bytes 6291456 | tf_op jit(solution)/shard_map/dot_general | solution.py:71
  5.4 6.3 %all_to_all.25 = f32[2,1024,256]{2,1,0:T(8,128)} all-to-all(f32[2,1024,256]{2,1,0:T(8,128)S(1)} %broadcast_in_dim.9), channel_id=1, replica_groups=mesh['row_0'=8,'row_1'=8,'row_2'=4,'col'=2] {'col'}, dimensions={0} | all-to-all | bytes 4194304 | tf_op jit(solution)/shard_map/all_to_all | solution.py:13
  11.8 1.8 %reduce_sum.29 = f32[1024,256]{1,0:T(8,128)S(1)} reduce(f32[2,1024,256]{2,1,0:T(8,128)} %all_to_all.25, f32[]{:T(128)} %constant.83.clone.1), dimensions={0}, to_apply=%region_0.0 | reduce | flops 262144 | bytes 3145732 | tf_op jit(solution)/shard_map/reduce_sum | solution.py:18
  13.6 1.3 copy.19
  14.9 1.5 %dot_general.14 = f32[64,4,1024]{2,1,0:T(4,128)S(1)} reshape(f32[256,1024]{1,0:T(8,128)} %copy.19) | data formatting | bytes 2097152 | tf_op jit(solution)/shard_map/dot_general | solution.py:73
  16.5 1.5 %convolution_bitcast_fusion = f32[4,64,1,256]{3,1,2,0:T(8,128)S(1)} fusion(f32[1024,256]{1,0:T(8,128)S(1)} %reduce_sum.29, f32[64,4,1024]{2,1,0:T(4,128)S(1)} %dot_general.14), kind=kOutput, calls=%fused_computation.3 | convolution fusion | flops 805306368 | bytes 2359296 | tf_op jit(solution)/shard_map/dot_general | solution.py:73
  18.0 11.1 %all_to_all.26 = f32[4,64,1,256]{3,1,2,0:T(8,128)S(1)} all-to-all(f32[4,64,1,256]{3,1,2,0:T(8,128)S(1)} %convolution_bitcast_fusion), channel_id=1, replica_groups=mesh['row_0'=8,'row_1'=8,'row_2'=4,'col'=2] {'row_2'}, dimensions={0} | all-to-all | bytes 524288 | tf_op jit(solution)/shard_map/all_to_all | solution.py:48
  29.2 27.8 %all_to_all.27 = f32[64,1,256]{2,1,0:T(1,128)S(1)} all-to-all(f32[64,1,256]{2,1,0:T(1,128)S(1)} %reduce_sum.31), channel_id=1, replica_groups=mesh['row_0'=8,'row_1'=8,'row_2'=4,'col'=2] {'row_0','row_1'}, dimensions={0} | all-to-all | bytes 131072 | tf_op jit(solution)/shard_map/all_to_all | solution.py:56
  57.7 5.4 %all-to-all-start.3 = ((f32[64,1,256]{2,1,0:T(1,128)}), f32[64,1,256]{2,1,0:T(1,128)S(1)}, u32[]{:S(2)}, u32[]{:S(2)}) async-start(f32[64,1,256]{2,1,0:T(1,128)} %broadcast_in_dim.10), calls=%async_computation.3 | async-start | bytes 131072 | tf_op jit(solution)/shard_map/all_to_all | solution.py:13
  63.1 11.5 %all-to-all-done.3 = f32[64,1,256]{2,1,0:T(1,128)S(1)} async-done(((f32[64,1,256]{2,1,0:T(1,128)}), f32[64,1,256]{2,1,0:T(1,128)S(1)}, u32[]{:S(2)}, u32[]{:S(2)}) %all-to-all-start.3) | async-done | bytes 65568 | tf_op jit(solution)/shard_map/all_to_all | solution.py:13
  74.6 0.7 broadcast_in_dim.12
  75.3 3.6 %all-to-all-start.4 = ((f32[4,64,1,256]{3,1,2,0:T(8,128)}), f32[4,64,1,256]{3,1,2,0:T(8,128)S(1)}, u32[]{:S(2)}, u32[]{:S(2)}) async-start(f32[4,64,1,256]{3,1,2,0:T(8,128)} %broadcast_in_dim.12), calls=%async_computation.4 | async-start | bytes 524288 | tf_op jit(solution)/shard_map/all_to_all | solution.py:13
  79.2 6.2 %all-to-all-done.4 = f32[4,64,1,256]{3,1,2,0:T(8,128)S(1)} async-done(((f32[4,64,1,256]{3,1,2,0:T(8,128)}), f32[4,64,1,256]{3,1,2,0:T(8,128)S(1)}, u32[]{:S(2)}, u32[]{:S(2)}) %all-to-all-start.4) | async-done | bytes 262176 | tf_op jit(solution)/shard_map/all_to_all | solution.py:13
  85.8 11.7 %cholesky.50 = f32[128,128]{1,0:T(8,128)S(1)} custom-call(f32[128,128]{1,0:T(8,128)S(1)} %cholesky.118), custom_call_target="Cholesky" | custom-call | tf_op jit(solution)/shard_map/jit(cholesky)/cholesky | solution.py:77
  97.6 9.8 %custom-call.15 = f32[1,128,128]{1,2,0:T(8,128)S(1)} custom-call(f32[1,128,128]{2,1,0:T(8,128)S(1)} %get-tuple-element.33), custom_call_target="InvertDiagBlocksLowerTriangular" | custom-call | tf_op jit(solution)/shard_map/jit(cholesky)/cholesky | solution.py:77
  107.9 11.7 %cholesky.105 = f32[128,128]{1,0:T(8,128)S(1)} custom-call(f32[128,128]{1,0:T(8,128)S(1)} %convolution_subtract_fusion.1), custom_call_target="Cholesky" | custom-call | tf_op jit(solution)/shard_map/jit(cholesky)/cholesky | solution.py:77
  119.7 0.7 compare_reduce_fusion
  121.9 4.1 %while.1 = (s32[]{:T(128)}, f32[256,256]{1,0:T(8,128)S(1)}, s32[2,2]{1,0:T(2,128)S(1)}, f32[2,128,128]{2,1,0:T(8,128)S(1)}, s32[]{:T(128)}) while((s32[]{:T(128)}, f32[256,256]{1,0:T(8,128)S(1)}, s32[2,2]{1,0:T(2,128)S(1)}, f32[2,128,128]{2,1,0:T(8,128)S(1)}, s32[]{:T(128)}) %tuple.32), condition=%wide.while_cond, body=%wide.while_body.sunk | while | flops 2 | bytes 131181 | solution.py:78
  122.5 1.4 bitcast_dynamic-update-slice_fusion.2
  124.5 1.4 bitcast_dynamic-update-slice_fusion.2
  126.0 19.9 %custom-call.16 = f32[2,128,128]{1,2,0:T(8,128)S(1)} custom-call(f32[2,128,128]{2,1,0:T(8,128)S(1)} %get-tuple-element.9), custom_call_target="InvertDiagBlocksLowerTriangular" | custom-call | tf_op jit(solution)/shard_map/jit(_solve_triangular)/triangular_solve | solution.py:78
  147.1 1.0 copy.25
  148.1 0.8 copy.26
  (32 shorter events, 4.8 us)
Async XLA Ops:
  0.6 1.2 copy-start
  57.7 16.9 %all-to-all-start.3 = ((f32[64,1,256]{2,1,0:T(1,128)}), f32[64,1,256]{2,1,0:T(1,128)S(1)}, u32[]{:S(2)}, u32[]{:S(2)}) async-start(f32[64,1,256]{2,1,0:T(1,128)} %broadcast_in_dim.10), calls=%async_computation.3 | async-start | bytes 131072 | tf_op jit(solution)/shard_map/all_to_all | solution.py:13
  75.3 10.1 %all-to-all-start.4 = ((f32[4,64,1,256]{3,1,2,0:T(8,128)}), f32[4,64,1,256]{3,1,2,0:T(8,128)S(1)}, u32[]{:S(2)}, u32[]{:S(2)}) async-start(f32[4,64,1,256]{3,1,2,0:T(8,128)} %broadcast_in_dim.12), calls=%async_computation.4 | async-start | bytes 524288 | tf_op jit(solution)/shard_map/all_to_all | solution.py:13
where the time goes:
time: 150 us; the launch traced here: 149 us
  other arithmetic  56 us (37%)
  blocking collectives  45.2 us (30%)
  waiting for transfers between devices  17.7 us (12%)
  local copies, waits for them, and re-layouts  12.3 us (8%)
  starting transfers between devices  8.94 us (6%)
  matrix products  6.65 us (4%)
  between operations  2.2 us (1%)
    another operation x6, other arithmetic, local(): factor = jnp.linalg.cholesky(gram).T  34 us
    all_to_all x1, blocking collectives, sum_by_axis(): lax.all_to_all(nearer, far, split_axis=0, concat_axis=0, tiled=True)  27.8 us
    another operation x2, other arithmetic, local(): basis = jax.scipy.linalg.solve_triangular(factor.T, block.T, lower=True).T  19.9 us
    all_to_all x2, waiting for transfers between devices, from_everyone(): lax.all_to_all(jnp.broadcast_to(x[None], (size, *x.shape)), axis, 0, 0, t...  17.7 us
    all_to_all x1, blocking collectives, sum_at_owner(): lax.all_to_all(blocks, axis, split_axis=0, concat_axis=0, tiled=True)  11.1 us
    all_to_all x2, starting transfers between devices, from_everyone(): lax.all_to_all(jnp.broadcast_to(x[None], (size, *x.shape)), axis, 0, 0, t...  8.94 us
    all_to_all x1, blocking collectives, from_everyone(): lax.all_to_all(jnp.broadcast_to(x[None], (size, *x.shape)), axis, 0, 0, t...  6.31 us
    another operation x6, local copies, waits for them, and re-layouts  4.06 us
  transfers between devices with their start and end apart: 2, of which 2 were waited for; matrix products, arithmetic and copies ran while one was open for 0% of the time, Pallas kernels for 0%

commit v1 on v0

v1 whole, which is shorter than its diff:
```python
import functools

import jax
import jax.numpy as jnp
from jax import lax
from jax.experimental import pallas as pl
from jax.experimental.pallas import tpu as pltpu
from jax.sharding import Mesh
from jax.sharding import PartitionSpec as P

ROW = ("z", "y", "x")
ROW_COL = ("z", "y", "x", "col")
SCATTER = ("z", "x")
SHARED = ("y", "col")
F32 = jnp.float32
HIGHEST = lax.Precision.HIGHEST
VMEM = pl.BlockSpec(memory_space=pltpu.VMEM)
HALF = 128
PACKED = 288
SMALL = pltpu.CompilerParams(vmem_limit_bytes=12 << 20)
LARGE = pltpu.CompilerParams(vmem_limit_bytes=63_500_288)


def dot(a, b, dim_a, dim_b):
    dims = (((dim_a,), (dim_b,)), ((), ()))
    return lax.dot_general(a, b, dims, precision=HIGHEST, preferred_element_type=F32)


def product_kernel(which_ref, panel_ref, sketch_ref, out_ref):
    out_ref[...] = jnp.dot(panel_ref[...], sketch_ref[...], preferred_element_type=F32)


def product(which, panel, sketch):
    rows, depth = panel.shape
    columns = sketch.shape[1]
    half, tile = rows // 2, 128
    steps = half // tile
    return pl.pallas_call(
        product_kernel,
        out_shape=jax.ShapeDtypeStruct((half, columns), F32),
        grid_spec=pltpu.PrefetchScalarGridSpec(
            num_scalar_prefetch=1,
            grid=(steps,),
            in_specs=[
                pl.BlockSpec((tile, depth), lambda i, which: (which[0] * steps + i, 0)),
                pl.BlockSpec((depth, columns), lambda i, which: (0, 0)),
            ],
            out_specs=pl.BlockSpec((tile, columns), lambda i, which: (i, 0)),
        ),
        cost_estimate=pl.CostEstimate(
            flops=2 * half * depth * columns,
            bytes_accessed=2 * (half + columns) * depth + 4 * half * columns,
            transcendentals=0,
        ),
        compiler_params=LARGE,
        name="product",
    )(which, panel, sketch)


def gram_kernel(own_ref, came_ref, block_ref, packed_ref):
    whole = own_ref[...] + came_ref[...]
    block_ref[...] = whole
    left, right = whole[:, :HALF], whole[:, HALF:]
    first = dot(left, left, 0, 0)
    packed_ref[HALF : 2 * HALF, :] = dot(left, right, 0, 0)
    last = dot(right, right, 0, 0)
    row = lax.broadcasted_iota(jnp.int32, (HALF, HALF), 0)
    lane = lax.broadcasted_iota(jnp.int32, (HALF, HALF), 1)
    packed_ref[:HALF, :] = jnp.where(lane >= row, first, last)
    diagonal = jnp.sum(jnp.where(lane == row, last, 0.0), axis=0, keepdims=True)
    packed_ref[2 * HALF :, :] = jnp.broadcast_to(diagonal, (PACKED - 2 * HALF, HALF))


def gram_of(own, came):
    return pl.pallas_call(
        gram_kernel,
        out_shape=(
            jax.ShapeDtypeStruct(own.shape, F32),
            jax.ShapeDtypeStruct((PACKED, HALF), F32),
        ),
        in_specs=[VMEM] * 2,
        out_specs=(VMEM, VMEM),
        compiler_params=SMALL,
        name="gram",
    )(own, came)


def sub(x, j):
    return jnp.broadcast_to(x[j : j + 1, :], (8, HALF))


def lane_of(x, j):
    return jnp.broadcast_to(x[:, j : j + 1], (8, HALF))


def eliminate(rows, extra):
    count = len(rows)
    rows, extra = list(rows), [list(e) for e in extra]
    sublane = lax.broadcasted_iota(jnp.int32, (8, HALF), 0)
    for g in range(count):
        c = [lane_of(rows[g], 8 * g + m) for m in range(8)]
        inverses, units, pivots = [], [], None
        for j in range(8):
            pivot = sub(c[j], j)
            pivots = pivot if j == 0 else jnp.where(sublane == j, pivot, pivots)
            inverse = 1.0 / pivot
            unit = c[j] * inverse
            for m in range(j + 1, 8):
                c[m] = c[m] - unit * sub(c[j], m)
            inverses.append(inverse)
            units.append(unit)
        parts = [rows[g]] + extra[g]
        for j in range(7):
            below = jnp.where(sublane > j, units[j], 0.0)
            parts = [x - below * sub(x, j) for x in parts]
        spread = [[sub(x, j) for x in parts] for j in range(8)]
        for h in range(g + 1, count):
            d = [lane_of(rows[h], 8 * g + m) for m in range(8)]
            lower = [rows[h]] + extra[h]
            for j in range(8):
                unit = d[j] * inverses[j]
                for m in range(j + 1, 8):
                    d[m] = d[m] - unit * sub(c[j], m)
                lower = [x - unit * b for x, b in zip(lower, spread[j])]
            rows[h], extra[h] = lower[0], lower[1:]
        scale = lax.rsqrt(pivots)
        parts = [x * scale for x in parts]
        rows[g], extra[g] = parts[0], parts[1:]
    return rows, extra


def factor_kernel(total_rows, packed_ref, block_ref, basis_ref, upper_ref, a11, a22, inv1, u12, inv2):
    row = lax.broadcasted_iota(jnp.int32, (HALF, HALF), 0)
    lane = lax.broadcasted_iota(jnp.int32, (HALF, HALF), 1)
    mixed = packed_ref[:HALF, :] / total_rows
    turned = mixed.T
    diagonal = packed_ref[2 * HALF : 2 * HALF + 1, :] / total_rows
    a11[...] = jnp.where(lane >= row, mixed, turned)
    a22[...] = jnp.where(lane == row, diagonal, jnp.where(lane < row, mixed, turned))
    sublane8 = lax.broadcasted_iota(jnp.int32, (8, HALF), 0)
    lane8 = lax.broadcasted_iota(jnp.int32, (8, HALF), 1)
    groups = [slice(8 * k, 8 * k + 8) for k in range(HALF // 8)]
    eye = [jnp.where(lane8 == sublane8 + 8 * k, 1.0, 0.0) for k in range(HALF // 8)]

    def kept(x, k):
        return jnp.where(lane8 >= sublane8 + 8 * k, x, 0.0)

    rows = [a11[at, :] for at in groups]
    extra = [
        [packed_ref[HALF + 8 * k : HALF + 8 * k + 8, :] / total_rows, eye[k]]
        for k in range(len(groups))
    ]
    rows, extra = eliminate(rows, extra)
    for k, at in enumerate(groups):
        upper_ref[at, :HALF] = kept(rows[k], k)
        upper_ref[at, HALF:] = extra[k][0]
        upper_ref[HALF + 8 * k : HALF + 8 * k + 8, :HALF] = jnp.zeros((8, HALF), F32)
        u12[at, :] = extra[k][0]
        inv1[at, :] = extra[k][1]
    across = u12[...]
    a22[...] = a22[...] - dot(across, across, 0, 0)
    first = dot(block_ref[:, :HALF], inv1[...], 1, 1)
    basis_ref[:, :HALF] = first
    rest = block_ref[:, HALF:] - dot(first, across, 1, 0)
    rows, extra = eliminate([a22[at, :] for at in groups], [[e] for e in eye])
    for k, at in enumerate(groups):
        upper_ref[HALF + 8 * k : HALF + 8 * k + 8, HALF:] = kept(rows[k], k)
        inv2[at, :] = extra[k][0]
    basis_ref[:, HALF:] = dot(rest, inv2[...], 1, 1)


def factor(total_rows, packed, block):
    return pl.pallas_call(
        functools.partial(factor_kernel, float(total_rows)),
        out_shape=(
            jax.ShapeDtypeStruct(block.shape, F32),
            jax.ShapeDtypeStruct((2 * HALF, 2 * HALF), F32),
        ),
        in_specs=[VMEM] * 2,
        out_specs=(VMEM, VMEM),
        scratch_shapes=[pltpu.VMEM((HALF, HALF), F32)] * 5,
        compiler_params=SMALL,
        name="factor",
    )(packed, block)


def exchanged(x, axis):
    return lax.all_to_all(x, axis, 0, 0, tiled=True)


def reduced(packed):
    owners, sharers = lax.axis_size(SCATTER), lax.axis_size(SHARED)
    pieces = packed.reshape(owners, 1, -1)
    mine = jnp.sum(exchanged(pieces, SCATTER), axis=0, keepdims=True)
    mine = jnp.broadcast_to(mine, (sharers, *mine.shape[1:]))
    mine = jnp.sum(exchanged(mine, SHARED), axis=0, keepdims=True)
    mine = jnp.broadcast_to(mine, (owners, *mine.shape[1:]))
    return exchanged(mine, SCATTER).reshape(packed.shape)


def local(panel, sketch):
    total_rows = panel.shape[0] * lax.axis_size(ROW)
    core = lax.axis_index("col").astype(jnp.int32).reshape(1)
    other = product(1 - core, panel, sketch)
    came = lax.ppermute(other, "col", [(0, 1), (1, 0)])
    own = product(core, panel, sketch)
    block, packed = gram_of(own, came)
    return factor(total_rows, reduced(packed), block)


def solution(mesh):
    sizes = (8, 8, 4, mesh.shape["col"])
    finer = Mesh(mesh.devices.reshape(sizes), ROW_COL)
    in_specs = (P(ROW, "col"), P("col", None))
    out_specs = (P(ROW_COL, None), P())
    return jax.shard_map(local, mesh=finer, in_specs=in_specs, out_specs=out_specs, check_vma=False)
```

time: 150 us -> 77.8 us (0.52)
  the two profiles are of different devices: /device:TPU:8 before, /device:TPU:1 now
where the time goes in v1:
time: 77.8 us; the launch traced here: 77.4 us
  blocking collectives  47.1 us (61%)
  Pallas kernels  19.6 us (25%)
  starting transfers between devices  8.73 us (11%)
  local copies, waits for them, and re-layouts  1.16 us (1%)
    all_to_all x3, blocking collectives, exchanged(): return lax.all_to_all(x, axis, 0, 0, tiled=True)  47.1 us
    pallas_call x1, Pallas kernels, factor(): pl.pallas_call(functools.partial(factor_kernel, float(total_rows)), out_s...  9.91 us
    pallas_call x2, Pallas kernels, product(): pl.pallas_call(product_kernel, out_shape=jax.ShapeDtypeStruct((half, colu...  8.82 us
    ppermute x1, starting transfers between devices, local(): came = lax.ppermute(other, 'col', [(0, 1), (1, 0)])  8.73 us
  transfers between devices with their start and end apart: 1, of which 0 were waited for; matrix products, arithmetic and copies ran while one was open for 0% of the time, Pallas kernels for 6%

profile of v1, /device:TPU:1, one launch (start us, length us, event | category | flops | bytes accessed | tf_op | source)
XLA Modules:
  0.0 77.4 jit_solution(13253711644736269314)
XLA Ops:
  0.6 4.4 %product.3 = f32[512,256]{1,0:T(8,128)} custom-call(s32[1]{0:T(128)S(6)} %sub.3.which_ref, bf16[1024,2048]{1,0:T(8,128)(2,1)} %panel_ref.3, bf16[2048,256]{1,0:T(8,128)(2,1)} %sketch_ref.3), custom_call_target="tpu_custom_call" | custom-call | flops 536870912 | bytes 3670016 | tf_op jit(solution)/shard_map/product/pallas_call | solution.py:38
  5.0 8.7 %collective-permute-start = (f32[512,256]{1,0:T(8,128)}, f32[512,256]{1,0:T(8,128)S(1)}, u32[]{:S(2)}, u32[]{:S(2)}) collective-permute-start(f32[512,256]{1,0:T(8,128)} %product.3), channel_id=1, source_target_pairs={{0,1},{1,0},{2,3},{3,2},{4,5},{5,4},{6,7},{7,6},{8,9},{9,8},{10,11... | collective-permute-start | bytes 1572872 | tf_op jit(solution)/shard_map/ppermute | solution.py:205
  13.8 4.4 %product.2.own_ref = f32[512,256]{1,0:T(8,128)} custom-call(s32[1]{0:T(128)} %bitcast.which_ref, bf16[1024,2048]{1,0:T(8,128)(2,1)} %panel_ref.3, bf16[2048,256]{1,0:T(8,128)(2,1)} %sketch_ref.3), custom_call_target="tpu_custom_call" | custom-call | flops 536870912 | bytes 3670016 | tf_op jit(solution)/shard_map/product/pallas_call | solution.py:38
  18.2 0.0 collective-permute-done.came_ref
  18.2 0.0 copy-start
  18.2 1.0 %copy-done = f32[512,256]{1,0:T(8,128)S(1)} copy-done((f32[512,256]{1,0:T(8,128)S(1)}, f32[512,256]{1,0:T(8,128)}, u32[]{:S(2)}) %copy-start) | copy-done | bytes 524312
  19.2 0.9 %gram.1 = (f32[512,256]{1,0:T(8,128)S(1)}, f32[288,128]{1,0:T(8,128)S(1)}) custom-call(f32[512,256]{1,0:T(8,128)S(1)} %copy-done, f32[512,256]{1,0:T(8,128)S(1)} %collective-permute-done.came_ref), custom_call_target="tpu_custom_call" | custom-call | tf_op jit(solution)/shard_map/gram/pallas_call | solution.py:75
  20.1 17.5 %all_to_all.15 = f32[32,1,1152]{2,1,0:T(1,128)S(1)} all-to-all(f32[32,1,1152]{2,1,0:T(1,128)S(1)} %bitcast.4), channel_id=1, replica_groups=mesh['z'=8,'y'=8,'x'=4,'col'=2] {'z','x'}, dimensions={0} | all-to-all | bytes 294912 | tf_op jit(solution)/shard_map/all_to_all | solution.py:188
  37.6 0.1 reduce_sum.18
  37.7 16.4 %all_to_all.16 = f32[16,1,1152]{2,1,0:T(1,128)S(1)} all-to-all(f32[16,1,1152]{2,1,0:T(1,128)S(1)} %broadcast_in_dim.4), channel_id=1, replica_groups=mesh['z'=8,'y'=8,'x'=4,'col'=2] {'y','col'}, dimensions={0} | all-to-all | bytes 147456 | tf_op jit(solution)/shard_map/all_to_all | solution.py:188
  54.1 0.1 reduce_sum.19
  54.2 0.1 broadcast_in_dim.5
  54.3 13.2 %all_to_all.17 = f32[32,1,1152]{2,1,0:T(1,128)S(1)} all-to-all(f32[32,1,1152]{2,1,0:T(1,128)S(1)} %broadcast_in_dim.5), channel_id=1, replica_groups=mesh['z'=8,'y'=8,'x'=4,'col'=2] {'z','x'}, dimensions={0} | all-to-all | bytes 294912 | tf_op jit(solution)/shard_map/all_to_all | solution.py:188
  67.5 9.9 %factor.1 = (f32[512,256]{1,0:T(8,128)}, f32[256,256]{1,0:T(8,128)}) custom-call(f32[288,128]{1,0:T(8,128)S(1)} %bitcast.3, f32[512,256]{1,0:T(8,128)S(1)} %get-tuple-element.5.block_ref), custom_call_target="tpu_custom_call" | custom-call | tf_op jit(solution)/shard_map/factor/pallas_call | solution.py:173
  (1 shorter events, 0.0 us)
Async XLA Ops:
  5.0 13.2 %collective-permute-start = (f32[512,256]{1,0:T(8,128)}, f32[512,256]{1,0:T(8,128)S(1)}, u32[]{:S(2)}, u32[]{:S(2)}) collective-permute-start(f32[512,256]{1,0:T(8,128)} %product.3), channel_id=1, source_target_pairs={{0,1},{1,0},{2,3},{3,2},{4,5},{5,4},{6,7},{7,6},{8,9},{9,8},{10,11... | collective-permute-start | bytes 1572872 | tf_op jit(solution)/shard_map/ppermute | solution.py:205
  18.2 1.0 %copy-start = (f32[512,256]{1,0:T(8,128)S(1)}, f32[512,256]{1,0:T(8,128)}, u32[]{:S(2)}) copy-start(f32[512,256]{1,0:T(8,128)} %product.2.own_ref) | copy-start | bytes 1572868

commit v2 on v1

v2 whole, which is shorter than its diff:
```python
import functools

import jax
import jax.numpy as jnp
from jax import lax
from jax.experimental import pallas as pl
from jax.experimental.pallas import tpu as pltpu
from jax.sharding import Mesh
from jax.sharding import PartitionSpec as P

ROW = ("z_hi", "z_lo", "y_hi", "y_lo", "x")
ROW_COL = (*ROW, "col")
SCATTER = ("z_lo", "y_lo", "x", "col")
SHARED = ("z_hi", "y_hi")
F32 = jnp.float32
HIGHEST = lax.Precision.HIGHEST
VMEM = pl.BlockSpec(memory_space=pltpu.VMEM)
HBM = pl.BlockSpec(memory_space=pltpu.HBM)
HALF = 128
PACKED = 288
SMALL = pltpu.CompilerParams(vmem_limit_bytes=12 << 20)
CHUNKS = 4


def dot(a, b, dim_a, dim_b):
    dims = (((dim_a,), (dim_b,)), ((), ()))
    return lax.dot_general(a, b, dims, precision=HIGHEST, preferred_element_type=F32)


def product_kernel(which_ref, panel_ref, sketch_ref, out_ref, rows, table, sems):
    half = out_ref.shape[0]
    depth = table.shape[0]
    start = pl.multiple_of(which_ref[0] * half, half)
    width = depth // CHUNKS
    copies = []
    for k in range(CHUNKS):
        at = slice(k * width, (k + 1) * width)
        sources = (sketch_ref.at[at, :], panel_ref.at[pl.ds(start, half), at])
        for n, (source, target) in enumerate(zip(sources, (table.at[at, :], rows.at[:, at]))):
            copies.append(pltpu.make_async_copy(source, target, sems.at[n, k]))
            copies[-1].start()
    for k in range(CHUNKS):
        at = slice(k * width, (k + 1) * width)
        copies[2 * k].wait()
        copies[2 * k + 1].wait()
        part = jnp.dot(rows[:, at], table[at, :], preferred_element_type=F32)
        out_ref[...] = part if k == 0 else out_ref[...] + part


def in_hbm(x):
    return pltpu.with_memory_space_constraint(x, pltpu.HBM)


def product(which, panel, sketch):
    rows, depth = panel.shape
    columns = sketch.shape[1]
    half = rows // 2
    return pl.pallas_call(
        product_kernel,
        out_shape=jax.ShapeDtypeStruct((half, columns), F32),
        in_specs=[pl.BlockSpec(memory_space=pltpu.SMEM), HBM, HBM],
        out_specs=VMEM,
        scratch_shapes=[
            pltpu.VMEM((half, depth), panel.dtype),
            pltpu.VMEM((depth, columns), sketch.dtype),
            pltpu.SemaphoreType.DMA((2, CHUNKS)),
        ],
        cost_estimate=pl.CostEstimate(
            flops=2 * half * depth * columns,
            bytes_accessed=2 * (half + columns) * depth + 4 * half * columns,
            transcendentals=0,
        ),
        compiler_params=SMALL,
        name="product",
    )(which, in_hbm(panel), in_hbm(sketch))


def gram_kernel(own_ref, came_ref, block_ref, packed_ref):
    whole = own_ref[...] + came_ref[...]
    block_ref[...] = whole
    left, right = whole[:, :HALF], whole[:, HALF:]
    first = dot(left, left, 0, 0)
    packed_ref[HALF : 2 * HALF, :] = dot(left, right, 0, 0)
    last = dot(right, right, 0, 0)
    row = lax.broadcasted_iota(jnp.int32, (HALF, HALF), 0)
    lane = lax.broadcasted_iota(jnp.int32, (HALF, HALF), 1)
    packed_ref[:HALF, :] = jnp.where(lane >= row, first, last)
    diagonal = jnp.sum(jnp.where(lane == row, last, 0.0), axis=0, keepdims=True)
    packed_ref[2 * HALF :, :] = jnp.broadcast_to(diagonal, (PACKED - 2 * HALF, HALF))


def gram_of(own, came):
    return pl.pallas_call(
        gram_kernel,
        out_shape=(
            jax.ShapeDtypeStruct(own.shape, F32),
            jax.ShapeDtypeStruct((PACKED, HALF), F32),
        ),
        in_specs=[VMEM] * 2,
        out_specs=(VMEM, VMEM),
        compiler_params=SMALL,
        name="gram",
    )(own, came)


def sub(x, j):
    return jnp.broadcast_to(x[j : j + 1, :], (8, HALF))


def lane_of(x, j):
    return jnp.broadcast_to(x[:, j : j + 1], (8, HALF))


def eliminate(work):
    sublane = lax.broadcasted_iota(jnp.int32, (8, HALF), 0)
    size, width = work.shape
    tiles = [slice(t, t + HALF) for t in range(0, width, HALF)]
    block = 16
    for first in range(0, size, block):
        count = min(4, (size - first) // 8)
        rows = [[work[first + 8 * g : first + 8 * g + 8, t] for t in tiles] for g in range(count)]
        cols = [
            [lane_of(rows[g][0], first + m) for m in range(block)]
            for g in range(count)
        ]
        for g in range(2):
            cols[g][0] = jnp.where(sublane < 8, cols[g][0], 0.0)
        pivots = [None, None]
        for j in range(block):
            home, at = divmod(j, 8)
            pivot = sub(cols[home][j], at)
            pivots[home] = pivot if at == 0 else jnp.where(sublane == at, pivot, pivots[home])
            inverse = 1.0 / pivot
            units = [cols[g][j] * inverse for g in range(count)]
            for m in range(j + 1, block):
                spread = sub(cols[m // 8][j], m % 8)
                for g in range(home, count):
                    if g < 2 and m >= 8 * (g + 1):
                        continue
                    cols[g][m] = cols[g][m] - units[g] * spread
            units[home] = jnp.where(sublane > at, units[home], 0.0)
            for t in range(len(tiles)):
                spread = sub(rows[home][t], at)
                for g in range(home, count):
                    rows[g][t] = rows[g][t] - units[g] * spread
        for g in range(count):
            scale = lax.rsqrt(pivots[g]) if g < 2 else None
            for t, tile in enumerate(tiles):
                x = rows[g][t] if scale is None else rows[g][t] * scale
                work[first + 8 * g : first + 8 * g + 8, tile] = x
        far = first + 2 * block
        if far < size:
            done = work[first : first + block, :]
            change = dot(done[:, :HALF], done, 0, 0)
            work[far:, :] = work[far:, :] - change[far:, :]


def factor_kernel(total_rows, packed_ref, block_ref, basis_ref, upper_ref, one, two, basis, upper, sems):
    row = lax.broadcasted_iota(jnp.int32, (HALF, HALF), 0)
    lane = lax.broadcasted_iota(jnp.int32, (HALF, HALF), 1)
    mixed = packed_ref[:HALF, :] / total_rows
    turned = mixed.T
    diagonal = packed_ref[2 * HALF : 2 * HALF + 1, :] / total_rows
    eye = jnp.where(lane == row, 1.0, 0.0)
    one[:, :HALF] = jnp.where(lane >= row, mixed, turned)
    one[:, HALF : 2 * HALF] = packed_ref[HALF : 2 * HALF, :] / total_rows
    one[:, 2 * HALF :] = eye
    two[:, :HALF] = jnp.where(lane == row, diagonal, jnp.where(lane < row, mixed, turned))
    two[:, HALF:] = eye
    eliminate(one)
    copies = []

    def send(source, target):
        copies.append(pltpu.make_async_copy(source, target, sems.at[len(copies)]))
        copies[-1].start()

    across = one[:, HALF : 2 * HALF]
    upper[:HALF, :HALF] = jnp.where(lane >= row, one[:, :HALF], 0.0)
    upper[:HALF, HALF:] = across
    upper[HALF:, :HALF] = jnp.zeros((HALF, HALF), F32)
    send(upper.at[:HALF], upper_ref.at[:HALF])
    two[:, :HALF] = two[:, :HALF] - dot(across, across, 0, 0)
    left = dot(block_ref[:, :HALF], one[:, 2 * HALF :], 1, 1)
    basis[:, :HALF] = left
    send(basis.at[:, :HALF], basis_ref.at[:, :HALF])
    rest = block_ref[:, HALF:] - dot(left, across, 1, 0)
    basis[:, HALF:] = rest
    eliminate(two)
    upper[HALF:, HALF:] = jnp.where(lane >= row, two[:, :HALF], 0.0)
    send(upper.at[HALF:], upper_ref.at[HALF:])
    quarter = block_ref.shape[0] // 4
    for k in range(4):
        at = slice(k * quarter, (k + 1) * quarter)
        basis[at, HALF:] = dot(basis[at, HALF:], two[:, HALF:], 1, 1)
        send(basis.at[at, HALF:], basis_ref.at[at, HALF:])
    for copy in copies:
        copy.wait()


def factor(total_rows, packed, block):
    return pl.pallas_call(
        functools.partial(factor_kernel, float(total_rows)),
        out_shape=(
            jax.ShapeDtypeStruct(block.shape, F32),
            jax.ShapeDtypeStruct((2 * HALF, 2 * HALF), F32),
        ),
        in_specs=[VMEM] * 2,
        out_specs=(HBM, HBM),
        scratch_shapes=[
            pltpu.VMEM((HALF, 3 * HALF), F32),
            pltpu.VMEM((HALF, 2 * HALF), F32),
            pltpu.VMEM(block.shape, F32),
            pltpu.VMEM((2 * HALF, 2 * HALF), F32),
            pltpu.SemaphoreType.DMA((7,)),
        ],
        compiler_params=SMALL,
        name="factor",
    )(packed, block)


def exchanged(x, axis):
    return lax.all_to_all(x, axis, 0, 0, tiled=True)


def reduced(packed):
    owners, sharers = lax.axis_size(SCATTER), lax.axis_size(SHARED)
    pieces = packed.reshape(owners, 1, -1)
    mine = jnp.sum(exchanged(pieces, SCATTER), axis=0, keepdims=True)
    mine = jnp.broadcast_to(mine, (sharers, *mine.shape[1:]))
    mine = jnp.sum(exchanged(mine, SHARED), axis=0, keepdims=True)
    mine = jnp.broadcast_to(mine, (owners, *mine.shape[1:]))
    return exchanged(mine, SCATTER).reshape(packed.shape)


def local(panel, sketch):
    total_rows = panel.shape[0] * lax.axis_size(ROW)
    core = lax.axis_index("col").astype(jnp.int32).reshape(1)
    other = product(1 - core, panel, sketch)
    came = lax.ppermute(other, "col", [(0, 1), (1, 0)])
    own = product(core, panel, sketch)
    block, packed = gram_of(own, came)
    return factor(total_rows, reduced(packed), block)


def solution(mesh):
    sizes = (4, 2, 4, 2, 4, mesh.shape["col"])
    finer = Mesh(mesh.devices.reshape(sizes), ROW_COL)
    in_specs = (P(ROW, "col"), P("col", None))
    out_specs = (P(ROW_COL, None), P())
    return jax.shard_map(local, mesh=finer, in_specs=in_specs, out_specs=out_specs, check_vma=False)
```

time: 77.8 us -> 69.5 us (0.89)
  Pallas kernels: 19.6 us -> 14 us
  blocking collectives: 47.1 us -> 45.5 us
  local copies, waits for them, and re-layouts: 1.16 us -> 0.12 us
    pallas_call x2, Pallas kernels: 8.82 us -> 5.31 us  [product(): pl.pallas_call(product_kernel, out_shape=jax.ShapeDtypeStruct((half, colu...]
    pallas_call x1, Pallas kernels: 9.91 us -> 7.85 us  [factor(): pl.pallas_call(functools.partial(factor_kernel, float(total_rows)), out_s...]
    all_to_all x3, blocking collectives: 47.1 us -> 45.5 us  [exchanged(): return lax.all_to_all(x, axis, 0, 0, tiled=True)]
    unnamed x2 -> x0, local copies, waits for them, and re-layouts: 1.04 us -> none
  transfers between devices with their start and end apart: 1 -> 1, of which waited for: 0 -> 0; matrix products, arithmetic and copies ran while one was open for 0% -> 0% of each run, Pallas kernels for 6% -> 4%
where the time goes in v2:
time: 69.5 us; the launch traced here: 69.3 us
  blocking collectives  45.5 us (65%)
  Pallas kernels  14 us (20%)
  starting transfers between devices  8.75 us (13%)
    all_to_all x3, blocking collectives, exchanged(): return lax.all_to_all(x, axis, 0, 0, tiled=True)  45.5 us
    ppermute x1, starting transfers between devices, local(): came = lax.ppermute(other, 'col', [(0, 1), (1, 0)])  8.75 us
    pallas_call x1, Pallas kernels, factor(): pl.pallas_call(functools.partial(factor_kernel, float(total_rows)), out_s...  7.85 us
    pallas_call x2, Pallas kernels, product(): pl.pallas_call(product_kernel, out_shape=jax.ShapeDtypeStruct((half, colu...  5.31 us
  transfers between devices with their start and end apart: 1, of which 0 were waited for; matrix products, arithmetic and copies ran while one was open for 0% of the time, Pallas kernels for 4%

profile of v2, /device:TPU:1, one launch (start us, length us, event | category | flops | bytes accessed | tf_op | source)
XLA Modules:
  0.0 69.3 jit_solution(13063478612919124978)
XLA Ops:
  0.6 2.7 %product.3 = f32[512,256]{1,0:T(8,128)S(1)} custom-call(s32[1]{0:T(128)S(6)} %sub.3.which_ref, bf16[1024,2048]{1,0:T(8,128)(2,1)} %panel_ref.3, bf16[2048,256]{1,0:T(8,128)(2,1)} %sketch_ref.3), custom_call_target="tpu_custom_call" | custom-call | flops 536870912 | bytes 3670016 | tf_op jit(solution)/shard_map/product/pallas_call | solution.py:58
  3.3 8.7 %collective-permute-start = (f32[512,256]{1,0:T(8,128)S(1)}, f32[512,256]{1,0:T(8,128)S(1)}, u32[]{:S(2)}, u32[]{:S(2)}) collective-permute-start(f32[512,256]{1,0:T(8,128)S(1)} %product.3), channel_id=1, source_target_pairs={{0,1},{1,0},{2,3},{3,2},{4,5},{5,4},{6,7},{7,6},{8,9},{9,8},{10,11... | collective-permute-start | bytes 1572872 | tf_op jit(solution)/shard_map/ppermute | solution.py:239
  12.0 2.7 %product.2.own_ref = f32[512,256]{1,0:T(8,128)S(1)} custom-call(s32[1]{0:T(128)} %bitcast.which_ref, bf16[1024,2048]{1,0:T(8,128)(2,1)} %panel_ref.3, bf16[2048,256]{1,0:T(8,128)(2,1)} %sketch_ref.3), custom_call_target="tpu_custom_call" | custom-call | flops 536870912 | bytes 3670016 | tf_op jit(solution)/shard_map/product/pallas_call | solution.py:58
  14.7 0.0 collective-permute-done.came_ref
  14.7 0.9 %gram.1 = (f32[512,256]{1,0:T(8,128)S(1)}, f32[288,128]{1,0:T(8,128)S(1)}) custom-call(f32[512,256]{1,0:T(8,128)S(1)} %product.2.own_ref, f32[512,256]{1,0:T(8,128)S(1)} %collective-permute-done.came_ref), custom_call_target="tpu_custom_call" | custom-call | tf_op jit(solution)/shard_map/gram/pallas_call | solution.py:93
  15.6 10.0 %all_to_all.15 = f32[32,1,1152]{2,1,0:T(1,128)S(1)} all-to-all(f32[32,1,1152]{2,1,0:T(1,128)S(1)} %bitcast.4), channel_id=1, replica_groups=mesh['z_hi'=4,'z_lo'=2,'y_hi'=4,'y_lo'=2,'x'=4,'col'=2] {'z_lo','y_lo','..., dimensions={0} | all-to-all | bytes 294912 | tf_op jit(solution)/shard_map/all_to_all | solution.py:222
  25.5 0.1 reduce_sum.18
  25.7 23.8 %all_to_all.16 = f32[16,1,1152]{2,1,0:T(1,128)S(1)} all-to-all(f32[16,1,1152]{2,1,0:T(1,128)S(1)} %broadcast_in_dim.4), channel_id=1, replica_groups=mesh['z_hi'=4,'z_lo'=2,'y_hi'=4,'y_lo'=2,'x'=4,'col'=2] {'z_hi','y_hi'}, dimensions={0} | all-to-all | bytes 147456 | tf_op jit(solution)/shard_map/all_to_all | solution.py:222
  49.5 0.1 reduce_sum.19
  49.6 0.1 broadcast_in_dim.5
  49.6 11.8 %all_to_all.17 = f32[32,1,1152]{2,1,0:T(1,128)S(1)} all-to-all(f32[32,1,1152]{2,1,0:T(1,128)S(1)} %broadcast_in_dim.5), channel_id=1, replica_groups=mesh['z_hi'=4,'z_lo'=2,'y_hi'=4,'y_lo'=2,'x'=4,'col'=2] {'z_lo','y_lo','..., dimensions={0} | all-to-all | bytes 294912 | tf_op jit(solution)/shard_map/all_to_all | solution.py:222
  61.4 7.9 %factor.1 = (f32[512,256]{1,0:T(8,128)}, f32[256,256]{1,0:T(8,128)}) custom-call(f32[288,128]{1,0:T(8,128)S(1)} %bitcast.3, f32[512,256]{1,0:T(8,128)S(1)} %get-tuple-element.5.block_ref), custom_call_target="tpu_custom_call" | custom-call | tf_op jit(solution)/shard_map/factor/pallas_call | solution.py:201
  (1 shorter events, 0.0 us)
Async XLA Ops:
  3.3 11.4 %collective-permute-start = (f32[512,256]{1,0:T(8,128)S(1)}, f32[512,256]{1,0:T(8,128)S(1)}, u32[]{:S(2)}, u32[]{:S(2)}) collective-permute-start(f32[512,256]{1,0:T(8,128)S(1)} %product.3), channel_id=1, source_target_pairs={{0,1},{1,0},{2,3},{3,2},{4,5},{5,4},{6,7},{7,6},{8,9},{9,8},{10,11... | collective-permute-start | bytes 1572872 | tf_op jit(solution)/shard_map/ppermute | solution.py:239

commit v3 on v2

--- a/solution.py
+++ b/solution.py
@@ -13,75 +13,134 @@
 SCATTER = ("z_lo", "y_lo", "x", "col")
 SHARED = ("z_hi", "y_hi")
 F32 = jnp.float32
-HIGHEST = lax.Precision.HIGHEST
+BF16 = jnp.bfloat16
 VMEM = pl.BlockSpec(memory_space=pltpu.VMEM)
 HBM = pl.BlockSpec(memory_space=pltpu.HBM)
 HALF = 128
 PACKED = 288
-SMALL = pltpu.CompilerParams(vmem_limit_bytes=12 << 20)
+SMEM = pl.BlockSpec(memory_space=pltpu.SMEM)
+SMALL = pltpu.CompilerParams(vmem_limit_bytes=16 << 20)
 CHUNKS = 4
 
 
+def pieces(x):
+    high = x.astype(BF16)
+    rest = x - high.astype(F32)
+    middle = rest.astype(BF16)
+    return high, middle, (rest - middle.astype(F32)).astype(BF16)
+
+
+def joined(x, dim, order):
+    parts = pieces(x)
+    return jnp.concatenate([parts[n] for n in order], axis=dim)
+
+
+LEFT, RIGHT = (0, 0, 0, 1, 1, 2), (0, 1, 2, 0, 1, 0)
+
+
+def bf16_dot(a, b, dim_a, dim_b):
+    dims = (((dim_a,), (dim_b,)), ((), ()))
+    return lax.dot_general(a, b, dims, preferred_element_type=F32)
+
+
 def dot(a, b, dim_a, dim_b):
-    dims = (((dim_a,), (dim_b,)), ((), ()))
-    return lax.dot_general(a, b, dims, precision=HIGHEST, preferred_element_type=F32)
-
-
-def product_kernel(which_ref, panel_ref, sketch_ref, out_ref, rows, table, sems):
-    half = out_ref.shape[0]
-    depth = table.shape[0]
-    start = pl.multiple_of(which_ref[0] * half, half)
+    return bf16_dot(joined(a, dim_a, LEFT), joined(b, dim_b, RIGHT), dim_a, dim_b)
+
+
+def other_kernel(core_ref, panel_ref, sketch_ref, out_ref, table_ref, ahead_ref, rows, sems):
+    half, depth = rows.shape
+    mine = pl.multiple_of(core_ref[0] * half, half)
+    other = pl.multiple_of((1 - core_ref[0]) * half, half)
     width = depth // CHUNKS
     copies = []
+
+    def fetch(source, target):
+        copies.append(pltpu.make_async_copy(source, target, sems.at[len(copies)]))
+        copies[-1].start()
+
     for k in range(CHUNKS):
         at = slice(k * width, (k + 1) * width)
-        sources = (sketch_ref.at[at, :], panel_ref.at[pl.ds(start, half), at])
-        for n, (source, target) in enumerate(zip(sources, (table.at[at, :], rows.at[:, at]))):
-            copies.append(pltpu.make_async_copy(source, target, sems.at[n, k]))
-            copies[-1].start()
+        fetch(sketch_ref.at[at, :], table_ref.at[at, :])
+        fetch(panel_ref.at[pl.ds(other, half), at], rows.at[:, at])
+    fetch(panel_ref.at[pl.ds(mine, ahead_ref.shape[0]), :], ahead_ref)
     for k in range(CHUNKS):
         at = slice(k * width, (k + 1) * width)
         copies[2 * k].wait()
         copies[2 * k + 1].wait()
-        part = jnp.dot(rows[:, at], table[at, :], preferred_element_type=F32)
+        part = jnp.dot(rows[:, at], table_ref[at, :], preferred_element_type=F32)
         out_ref[...] = part if k == 0 else out_ref[...] + part
+    copies[-1].wait()
+
+
+def own_kernel(core_ref, panel_ref, table_ref, ahead_ref, out_ref, rows, sem):
+    early, late = ahead_ref.shape[0], rows.shape[0]
+    start = pl.multiple_of(core_ref[0] * (early + late) + early, early)
+    copy = pltpu.make_async_copy(panel_ref.at[pl.ds(start, late), :], rows, sem)
+    copy.start()
+    out_ref[:early, :] = jnp.dot(ahead_ref[...], table_ref[...], preferred_element_type=F32)
+    copy.wait()
+    out_ref[early:, :] = jnp.dot(rows[...], table_ref[...], preferred_element_type=F32)
 
 
 def in_hbm(x):
     return pltpu.with_memory_space_constraint(x, pltpu.HBM)
 
 
-def product(which, panel, sketch):
+def cost(rows, depth, columns, fetched):
+    return pl.CostEstimate(
+        flops=2 * rows * depth * columns,
+        bytes_accessed=2 * fetched * depth + 4 * rows * columns,
+        transcendentals=0,
+    )
+
+
+def other_product(core, panel, sketch):
     rows, depth = panel.shape
     columns = sketch.shape[1]
-    half = rows // 2
+    half, ahead = rows // 2, rows // 4
     return pl.pallas_call(
-        product_kernel,
-        out_shape=jax.ShapeDtypeStruct((half, columns), F32),
-        in_specs=[pl.BlockSpec(memory_space=pltpu.SMEM), HBM, HBM],
-        out_specs=VMEM,
+        other_kernel,
+        out_shape=(
+            jax.ShapeDtypeStruct((half, columns), F32),
+            jax.ShapeDtypeStruct(sketch.shape, sketch.dtype),
+            jax.ShapeDtypeStruct((ahead, depth), panel.dtype),
+        ),
+        in_specs=[SMEM, HBM, HBM],
+        out_specs=(VMEM, VMEM, VMEM),
         scratch_shapes=[
             pltpu.VMEM((half, depth), panel.dtype),
-            pltpu.VMEM((depth, columns), sketch.dtype),
-            pltpu.SemaphoreType.DMA((2, CHUNKS)),
+            pltpu.SemaphoreType.DMA((2 * CHUNKS + 1,)),
         ],
-        cost_estimate=pl.CostEstimate(
-            flops=2 * half * depth * columns,
-            bytes_accessed=2 * (half + columns) * depth + 4 * half * columns,
-            transcendentals=0,
-        ),
+        cost_estimate=cost(half, depth, columns, half + ahead + columns),
         compiler_params=SMALL,
-        name="product",
-    )(which, in_hbm(panel), in_hbm(sketch))
+        name="other_product",
+    )(core, in_hbm(panel), in_hbm(sketch))
+
+
+def own_product(core, panel, table, ahead):
+    depth, columns = table.shape
+    half = panel.shape[0] // 2
+    late = half - ahead.shape[0]
+    return pl.pallas_call(
+        own_kernel,
+        out_shape=jax.ShapeDtypeStruct((half, columns), F32),
+        in_specs=[SMEM, HBM, VMEM, VMEM],
+        out_specs=VMEM,
+        scratch_shapes=[pltpu.VMEM((late, depth), panel.dtype), pltpu.SemaphoreType.DMA],
+        cost_estimate=cost(half, depth, columns, late),
+        compiler_params=SMALL,
+        name="own_product",
+    )(core, in_hbm(panel), table, ahead)
 
 
 def gram_kernel(own_ref, came_ref, block_ref, packed_ref):
     whole = own_ref[...] + came_ref[...]
     block_ref[...] = whole
-    left, right = whole[:, :HALF], whole[:, HALF:]
-    first = dot(left, left, 0, 0)
-    packed_ref[HALF : 2 * HALF, :] = dot(left, right, 0, 0)
-    last = dot(right, right, 0, 0)
+    left, right = joined(whole, 0, LEFT), joined(whole, 0, RIGHT)
+    top = bf16_dot(left[:, :HALF], right, 0, 0)
+    first = top[:, :HALF]
+    packed_ref[HALF : 2 * HALF, :] = top[:, HALF:]
+    last = bf16_dot(left[:, HALF:], right[:, HALF:], 0, 0)
     row = lax.broadcasted_iota(jnp.int32, (HALF, HALF), 0)
     lane = lax.broadcasted_iota(jnp.int32, (HALF, HALF), 1)
     packed_ref[:HALF, :] = jnp.where(lane >= row, first, last)
@@ -235,9 +294,9 @@
 def local(panel, sketch):
     total_rows = panel.shape[0] * lax.axis_size(ROW)
     core = lax.axis_index("col").astype(jnp.int32).reshape(1)
-    other = product(1 - core, panel, sketch)
+    other, table, ahead = other_product(core, panel, sketch)
     came = lax.ppermute(other, "col", [(0, 1), (1, 0)])
-    own = product(core, panel, sketch)
+    own = own_product(core, panel, table, ahead)
     block, packed = gram_of(own, came)
     return factor(total_rows, reduced(packed), block)
 

time: 69.5 us -> 67.1 us (0.965)
  Pallas kernels: 14 us -> 11.5 us
    pallas_call x1, Pallas kernels: 7.85 us -> 6.3 us  [factor(): pl.pallas_call(functools.partial(factor_kernel, float(total_rows)), out_s...]
  transfers between devices with their start and end apart: 1 -> 1, of which waited for: 0 -> 0; matrix products, arithmetic and copies ran while one was open for 0% -> 0% of each run, Pallas kernels for 4% -> 3%
where the time goes in v3:
time: 67.1 us; the launch traced here: 66.8 us
  blocking collectives  45.6 us (68%)
  Pallas kernels  11.5 us (17%)
  starting transfers between devices  8.75 us (13%)
  between operations  0.69 us (1%)
    all_to_all x3, blocking collectives, exchanged(): return lax.all_to_all(x, axis, 0, 0, tiled=True)  45.6 us
    ppermute x1, starting transfers between devices, local(): came = lax.ppermute(other, 'col', [(0, 1), (1, 0)])  8.75 us
    pallas_call x1, Pallas kernels, factor(): pl.pallas_call(functools.partial(factor_kernel, float(total_rows)), out_s...  6.3 us
    pallas_call x1, Pallas kernels, other_product(): pl.pallas_call(other_kernel, out_shape=(jax.ShapeDtypeStruct((half, colum...  2.68 us
    pallas_call x1, Pallas kernels, own_product(): pl.pallas_call(own_kernel, out_shape=jax.ShapeDtypeStruct((half, columns)...  1.93 us
  transfers between devices with their start and end apart: 1, of which 0 were waited for; matrix products, arithmetic and copies ran while one was open for 0% of the time, Pallas kernels for 3%

profile of v3, /device:TPU:1, one launch (start us, length us, event | category | flops | bytes accessed | tf_op | source)
XLA Modules:
  0.0 66.8 jit_solution(10702196483008937386)
XLA Ops:
  0.6 2.7 %other_product.1 = (f32[512,256]{1,0:T(8,128)S(1)}, bf16[2048,256]{1,0:T(8,128)(2,1)S(1)}, bf16[256,2048]{1,0:T(8,128)(2,1)S(1)}) custom-call(s32[1]{0:T(128)} %bitcast.core_ref, bf16[1024,2048]{1,0:T(8,128)(2,1)} %panel_ref.3, bf16[2048,256]{1,0:T(8,128)(2,1)} %sketch_ref.1), custom_call_target="tpu_custom_call" | custom-call | flops 536870912 | bytes 4718592 | tf_op jit(solution)/shard_map/other_product/pallas_call | solution.py:101
  3.3 8.7 %collective-permute-start = (f32[512,256]{1,0:T(8,128)S(1)}, f32[512,256]{1,0:T(8,128)S(1)}, u32[]{:S(2)}, u32[]{:S(2)}) collective-permute-start(f32[512,256]{1,0:T(8,128)S(1)} %get-tuple-element.9), channel_id=1, source_target_pairs={{0,1},{1,0},{2,3},{3,2},{4,5},{5,4},{6,7},{7,6},{8,9},{9,8},{10,11... | collective-permute-start | bytes 1572872 | tf_op jit(solution)/shard_map/ppermute | solution.py:298
  12.1 1.9 %own_product.1.own_ref = f32[512,256]{1,0:T(8,128)S(1)} custom-call(s32[1]{0:T(128)} %bitcast.core_ref, bf16[1024,2048]{1,0:T(8,128)(2,1)} %panel_ref.3, bf16[2048,256]{1,0:T(8,128)(2,1)S(1)} %get-tuple-element.7.table_ref, bf16[256,2048]{1,0:T(8,128)(2,1)S(1)} %get-tuple-element.8.ahead_ref), custom_call_target="tpu_custom_call" | custom-call | flops 536870912 | bytes 1572864 | tf_op jit(solution)/shard_map/own_product/pallas_call | solution.py:124
  14.0 0.0 collective-permute-done.came_ref
  14.0 0.6 gram.1
  14.6 10.0 %all_to_all.15 = f32[32,1,1152]{2,1,0:T(1,128)S(1)} all-to-all(f32[32,1,1152]{2,1,0:T(1,128)S(1)} %bitcast.4), channel_id=1, replica_groups=mesh['z_hi'=4,'z_lo'=2,'y_hi'=4,'y_lo'=2,'x'=4,'col'=2] {'z_lo','y_lo','..., dimensions={0} | all-to-all | bytes 294912 | tf_op jit(solution)/shard_map/all_to_all | solution.py:281
  24.6 0.1 reduce_sum.18
  24.8 23.8 %all_to_all.16 = f32[16,1,1152]{2,1,0:T(1,128)S(1)} all-to-all(f32[16,1,1152]{2,1,0:T(1,128)S(1)} %broadcast_in_dim.4), channel_id=1, replica_groups=mesh['z_hi'=4,'z_lo'=2,'y_hi'=4,'y_lo'=2,'x'=4,'col'=2] {'z_hi','y_hi'}, dimensions={0} | all-to-all | bytes 147456 | tf_op jit(solution)/shard_map/all_to_all | solution.py:281
  48.6 0.1 reduce_sum.19
  48.6 0.1 broadcast_in_dim.5
  48.7 11.8 %all_to_all.17 = f32[32,1,1152]{2,1,0:T(1,128)S(1)} all-to-all(f32[32,1,1152]{2,1,0:T(1,128)S(1)} %broadcast_in_dim.5), channel_id=1, replica_groups=mesh['z_hi'=4,'z_lo'=2,'y_hi'=4,'y_lo'=2,'x'=4,'col'=2] {'z_lo','y_lo','..., dimensions={0} | all-to-all | bytes 294912 | tf_op jit(solution)/shard_map/all_to_all | solution.py:281
  60.5 6.3 %factor.1 = (f32[512,256]{1,0:T(8,128)}, f32[256,256]{1,0:T(8,128)}) custom-call(f32[288,128]{1,0:T(8,128)S(1)} %bitcast.3, f32[512,256]{1,0:T(8,128)S(1)} %get-tuple-element.11.block_ref), custom_call_target="tpu_custom_call" | custom-call | tf_op jit(solution)/shard_map/factor/pallas_call | solution.py:260
  (1 shorter events, 0.0 us)
Async XLA Ops:
  3.3 10.7 %collective-permute-start = (f32[512,256]{1,0:T(8,128)S(1)}, f32[512,256]{1,0:T(8,128)S(1)}, u32[]{:S(2)}, u32[]{:S(2)}) collective-permute-start(f32[512,256]{1,0:T(8,128)S(1)} %get-tuple-element.9), channel_id=1, source_target_pairs={{0,1},{1,0},{2,3},{3,2},{4,5},{5,4},{6,7},{7,6},{8,9},{9,8},{10,11... | collective-permute-start | bytes 1572872 | tf_op jit(solution)/shard_map/ppermute | solution.py:298

commit v4 on v3

--- a/solution.py
+++ b/solution.py
@@ -11,13 +11,14 @@
 ROW = ("z_hi", "z_lo", "y_hi", "y_lo", "x")
 ROW_COL = (*ROW, "col")
 SCATTER = ("z_lo", "y_lo", "x", "col")
-SHARED = ("z_hi", "y_hi")
+SHARED = ("z_hi", "z_lo", "y_hi", "y_lo")
 F32 = jnp.float32
 BF16 = jnp.bfloat16
 VMEM = pl.BlockSpec(memory_space=pltpu.VMEM)
 HBM = pl.BlockSpec(memory_space=pltpu.HBM)
 HALF = 128
 PACKED = 288
+QUARTERS = 4
 SMEM = pl.BlockSpec(memory_space=pltpu.SMEM)
 SMALL = pltpu.CompilerParams(vmem_limit_bytes=16 << 20)
 CHUNKS = 4
@@ -133,7 +134,7 @@
     )(core, in_hbm(panel), table, ahead)
 
 
-def gram_kernel(own_ref, came_ref, block_ref, packed_ref):
+def gram_kernel(turn_ref, own_ref, came_ref, block_ref, placed_ref, packed_ref):
     whole = own_ref[...] + came_ref[...]
     block_ref[...] = whole
     left, right = joined(whole, 0, LEFT), joined(whole, 0, RIGHT)
@@ -146,20 +147,32 @@
     packed_ref[:HALF, :] = jnp.where(lane >= row, first, last)
     diagonal = jnp.sum(jnp.where(lane == row, last, 0.0), axis=0, keepdims=True)
     packed_ref[2 * HALF :, :] = jnp.broadcast_to(diagonal, (PACKED - 2 * HALF, HALF))
-
-
-def gram_of(own, came):
+    for k in range(QUARTERS):
+        placed_ref[owners_place(turn_ref, k), :] = packed_ref[quarter(k), :]
+
+
+def quarter(k):
+    return slice(k * PACKED // QUARTERS, (k + 1) * PACKED // QUARTERS)
+
+
+def owners_place(turn_ref, k):
+    rows = PACKED // QUARTERS
+    return pl.ds(pl.multiple_of((k ^ turn_ref[0]) * rows, 8), rows)
+
+
+def gram_of(turn, own, came):
     return pl.pallas_call(
         gram_kernel,
         out_shape=(
             jax.ShapeDtypeStruct(own.shape, F32),
             jax.ShapeDtypeStruct((PACKED, HALF), F32),
         ),
-        in_specs=[VMEM] * 2,
+        in_specs=[SMEM, VMEM, VMEM],
         out_specs=(VMEM, VMEM),
+        scratch_shapes=[pltpu.VMEM((PACKED, HALF), F32)],
         compiler_params=SMALL,
         name="gram",
-    )(own, came)
+    )(turn, own, came)
 
 
 def sub(x, j):
@@ -176,7 +189,9 @@
     tiles = [slice(t, t + HALF) for t in range(0, width, HALF)]
     block = 16
     for first in range(0, size, block):
-        count = min(4, (size - first) // 8)
+        left = (size - first - block) // 8
+        look = left if left <= 4 else 3
+        count = 2 + look
         rows = [[work[first + 8 * g : first + 8 * g + 8, t] for t in tiles] for g in range(count)]
         cols = [
             [lane_of(rows[g][0], first + m) for m in range(block)]
@@ -207,14 +222,18 @@
             for t, tile in enumerate(tiles):
                 x = rows[g][t] if scale is None else rows[g][t] * scale
                 work[first + 8 * g : first + 8 * g + 8, tile] = x
-        far = first + 2 * block
+        far = first + block + 8 * look
         if far < size:
             done = work[first : first + block, :]
             change = dot(done[:, :HALF], done, 0, 0)
             work[far:, :] = work[far:, :] - change[far:, :]
 
 
-def factor_kernel(total_rows, packed_ref, block_ref, basis_ref, upper_ref, one, two, basis, upper, sems):
+def factor_kernel(
+    total_rows, turn_ref, placed_ref, block_ref, basis_ref, upper_ref, packed_ref, one, two, basis, upper, sems
+):
+    for k in range(QUARTERS):
+        packed_ref[quarter(k), :] = placed_ref[owners_place(turn_ref, k), :]
     row = lax.broadcasted_iota(jnp.int32, (HALF, HALF), 0)
     lane = lax.broadcasted_iota(jnp.int32, (HALF, HALF), 1)
     mixed = packed_ref[:HALF, :] / total_rows
@@ -247,25 +266,26 @@
     eliminate(two)
     upper[HALF:, HALF:] = jnp.where(lane >= row, two[:, :HALF], 0.0)
     send(upper.at[HALF:], upper_ref.at[HALF:])
-    quarter = block_ref.shape[0] // 4
+    strip = block_ref.shape[0] // 4
     for k in range(4):
-        at = slice(k * quarter, (k + 1) * quarter)
+        at = slice(k * strip, (k + 1) * strip)
         basis[at, HALF:] = dot(basis[at, HALF:], two[:, HALF:], 1, 1)
         send(basis.at[at, HALF:], basis_ref.at[at, HALF:])
     for copy in copies:
         copy.wait()
 
 
-def factor(total_rows, packed, block):
+def factor(total_rows, turn, placed, block):
     return pl.pallas_call(
         functools.partial(factor_kernel, float(total_rows)),
         out_shape=(
             jax.ShapeDtypeStruct(block.shape, F32),
             jax.ShapeDtypeStruct((2 * HALF, 2 * HALF), F32),
         ),
-        in_specs=[VMEM] * 2,
+        in_specs=[SMEM, VMEM, VMEM],
         out_specs=(HBM, HBM),
         scratch_shapes=[
+            pltpu.VMEM((PACKED, HALF), F32),
             pltpu.VMEM((HALF, 3 * HALF), F32),
             pltpu.VMEM((HALF, 2 * HALF), F32),
             pltpu.VMEM(block.shape, F32),
@@ -274,21 +294,38 @@
         ],
         compiler_params=SMALL,
         name="factor",
-    )(packed, block)
-
-
-def exchanged(x, axis):
-    return lax.all_to_all(x, axis, 0, 0, tiled=True)
-
-
-def reduced(packed):
-    owners, sharers = lax.axis_size(SCATTER), lax.axis_size(SHARED)
-    pieces = packed.reshape(owners, 1, -1)
+    )(turn, placed, block)
+
+
+def turned(high):
+    return 1 - (((high + 1) >> 1) & 1)
+
+
+def sharers():
+    z_pairs, y_pairs = lax.axis_size("z_hi"), lax.axis_size("y_hi")
+    return [
+        [
+            ((z * 2 + (i ^ turned(z))) * y_pairs + y) * 2 + (j ^ turned(y))
+            for z in range(z_pairs)
+            for y in range(y_pairs)
+        ]
+        for i in range(2)
+        for j in range(2)
+    ]
+
+
+def exchanged(x, axis, groups=None):
+    return lax.all_to_all(x, axis, 0, 0, axis_index_groups=groups, tiled=True)
+
+
+def reduced(placed):
+    owners, groups = lax.axis_size(SCATTER), sharers()
+    pieces = placed.reshape(owners, 1, -1)
     mine = jnp.sum(exchanged(pieces, SCATTER), axis=0, keepdims=True)
-    mine = jnp.broadcast_to(mine, (sharers, *mine.shape[1:]))
-    mine = jnp.sum(exchanged(mine, SHARED), axis=0, keepdims=True)
+    mine = jnp.broadcast_to(mine, (len(groups[0]), *mine.shape[1:]))
+    mine = jnp.sum(exchanged(mine, SHARED, groups), axis=0, keepdims=True)
     mine = jnp.broadcast_to(mine, (owners, *mine.shape[1:]))
-    return exchanged(mine, SCATTER).reshape(packed.shape)
+    return exchanged(mine, SCATTER).reshape(placed.shape)
 
 
 def local(panel, sketch):
@@ -297,8 +334,10 @@
     other, table, ahead = other_product(core, panel, sketch)
     came = lax.ppermute(other, "col", [(0, 1), (1, 0)])
     own = own_product(core, panel, table, ahead)
-    block, packed = gram_of(own, came)
-    return factor(total_rows, reduced(packed), block)
+    turn = 2 * turned(lax.axis_index("z_hi")) + turned(lax.axis_index("y_hi"))
+    turn = turn.astype(jnp.int32).reshape(1)
+    block, placed = gram_of(turn, own, came)
+    return factor(total_rows, turn, reduced(placed), block)
 
 
 def solution(mesh):

time: 67.1 us -> 65.3 us (0.973)
  blocking collectives: 45.6 us -> 43.9 us
    all_to_all x3, blocking collectives: 45.6 us -> 43.9 us  [exchanged(): return lax.all_to_all(x, axis, 0, 0, axis_index_groups=groups, tiled=True)]
where the time goes in v4:
time: 65.3 us; the launch traced here: 65 us
  blocking collectives  43.9 us (67%)
  Pallas kernels  11.4 us (17%)
  starting transfers between devices  8.75 us (13%)
  between operations  0.7 us (1%)
    all_to_all x3, blocking collectives, exchanged(): return lax.all_to_all(x, axis, 0, 0, axis_index_groups=groups, tiled=True)  43.9 us
    ppermute x1, starting transfers between devices, local(): came = lax.ppermute(other, 'col', [(0, 1), (1, 0)])  8.75 us
    pallas_call x1, Pallas kernels, factor(): pl.pallas_call(functools.partial(factor_kernel, float(total_rows)), out_s...  6.16 us
    pallas_call x1, Pallas kernels, other_product(): pl.pallas_call(other_kernel, out_shape=(jax.ShapeDtypeStruct((half, colum...  2.66 us
    pallas_call x1, Pallas kernels, own_product(): pl.pallas_call(own_kernel, out_shape=jax.ShapeDtypeStruct((half, columns)...  1.93 us
  transfers between devices with their start and end apart: 1, of which 0 were waited for; matrix products, arithmetic and copies ran while one was open for 0% of the time, Pallas kernels for 3%

profile of v4, /device:TPU:1, one launch (start us, length us, event | category | flops | bytes accessed | tf_op | source)
XLA Modules:
  0.0 65.0 jit_solution(7078038696041779892)
XLA Ops:
  0.6 2.7 %other_product.1 = (f32[512,256]{1,0:T(8,128)S(1)}, bf16[2048,256]{1,0:T(8,128)(2,1)S(1)}, bf16[256,2048]{1,0:T(8,128)(2,1)S(1)}) custom-call(s32[1]{0:T(128)} %bitcast.1.core_ref, bf16[1024,2048]{1,0:T(8,128)(2,1)} %panel_ref.3, bf16[2048,256]{1,0:T(8,128)(2,1)} %sketch_ref.1), custom_call_target="tpu_custom_call" | custom-call | flops 536870912 | bytes 4718592 | tf_op jit(solution)/shard_map/other_product/pallas_call | solution.py:102
  3.3 8.7 %collective-permute-start = (f32[512,256]{1,0:T(8,128)S(1)}, f32[512,256]{1,0:T(8,128)S(1)}, u32[]{:S(2)}, u32[]{:S(2)}) collective-permute-start(f32[512,256]{1,0:T(8,128)S(1)} %get-tuple-element.9), channel_id=1, source_target_pairs={{0,1},{1,0},{2,3},{3,2},{4,5},{5,4},{6,7},{7,6},{8,9},{9,8},{10,11... | collective-permute-start | bytes 1572872 | tf_op jit(solution)/shard_map/ppermute | solution.py:335
  12.1 1.9 %own_product.1.own_ref = f32[512,256]{1,0:T(8,128)S(1)} custom-call(s32[1]{0:T(128)} %bitcast.1.core_ref, bf16[1024,2048]{1,0:T(8,128)(2,1)} %panel_ref.3, bf16[2048,256]{1,0:T(8,128)(2,1)S(1)} %get-tuple-element.7.table_ref, bf16[256,2048]{1,0:T(8,128)(2,1)S(1)} %get-tuple-element.8.ahead_ref), custom_call_target="tpu_custom_call" | custom-call | flops 536870912 | bytes 1572864 | tf_op jit(solution)/shard_map/own_product/pallas_call | solution.py:125
  14.0 0.0 collective-permute-done.came_ref
  14.0 0.6 gram.1
  14.7 10.0 %all_to_all.15 = f32[32,1,1152]{2,1,0:T(1,128)S(1)} all-to-all(f32[32,1,1152]{2,1,0:T(1,128)S(1)} %bitcast.5), channel_id=1, replica_groups=mesh['z_hi'=4,'z_lo'=2,'y_hi'=4,'y_lo'=2,'x'=4,'col'=2] {'z_lo','y_lo','..., dimensions={0} | all-to-all | bytes 294912 | tf_op jit(solution)/shard_map/all_to_all | solution.py:318
  24.6 0.1 reduce_sum.18
  24.8 21.2 %all_to_all.16 = f32[16,1,1152]{2,1,0:T(1,128)S(1)} all-to-all(f32[16,1,1152]{2,1,0:T(1,128)S(1)} %broadcast_in_dim.4), channel_id=1, replica_groups={{72,80,96,120,136,144,160,184,264,272,288,312,456,464,480,504},{64,88,1..., dimensions={0} | all-to-all | bytes 147456 | tf_op jit(solution)/shard_map/all_to_all | solution.py:318
  46.0 0.1 reduce_sum.19
  46.0 0.1 broadcast_in_dim.5
  46.1 12.8 %all_to_all.17 = f32[32,1,1152]{2,1,0:T(1,128)S(1)} all-to-all(f32[32,1,1152]{2,1,0:T(1,128)S(1)} %broadcast_in_dim.5), channel_id=1, replica_groups=mesh['z_hi'=4,'z_lo'=2,'y_hi'=4,'y_lo'=2,'x'=4,'col'=2] {'z_lo','y_lo','..., dimensions={0} | all-to-all | bytes 294912 | tf_op jit(solution)/shard_map/all_to_all | solution.py:318
  58.9 6.2 %factor.1 = (f32[512,256]{1,0:T(8,128)}, f32[256,256]{1,0:T(8,128)}) custom-call(s32[1]{0:T(128)} %bitcast.turn_ref, f32[288,128]{1,0:T(8,128)S(1)} %bitcast.4, f32[512,256]{1,0:T(8,128)S(1)} %get-tuple-element.11.block_ref), custom_call_target="tpu_custom_call" | custom-call | tf_op jit(solution)/shard_map/factor/pallas_call | solution.py:279
  (1 shorter events, 0.0 us)
Async XLA Ops:
  3.3 10.7 %collective-permute-start = (f32[512,256]{1,0:T(8,128)S(1)}, f32[512,256]{1,0:T(8,128)S(1)}, u32[]{:S(2)}, u32[]{:S(2)}) collective-permute-start(f32[512,256]{1,0:T(8,128)S(1)} %get-tuple-element.9), channel_id=1, source_target_pairs={{0,1},{1,0},{2,3},{3,2},{4,5},{5,4},{6,7},{7,6},{8,9},{9,8},{10,11... | collective-permute-start | bytes 1572872 | tf_op jit(solution)/shard_map/ppermute | solution.py:335

commit v5 on v4

--- a/solution.py
+++ b/solution.py
@@ -21,7 +21,7 @@
 QUARTERS = 4
 SMEM = pl.BlockSpec(memory_space=pltpu.SMEM)
 SMALL = pltpu.CompilerParams(vmem_limit_bytes=16 << 20)
-CHUNKS = 4
+CHUNKS = (3, 3, 2)
 
 
 def pieces(x):
@@ -52,20 +52,20 @@
     half, depth = rows.shape
     mine = pl.multiple_of(core_ref[0] * half, half)
     other = pl.multiple_of((1 - core_ref[0]) * half, half)
-    width = depth // CHUNKS
+    unit = depth // sum(CHUNKS)
+    ends = [unit * sum(CHUNKS[:k]) for k in range(len(CHUNKS) + 1)]
+    chunks = [slice(*at) for at in zip(ends, ends[1:])]
     copies = []
 
     def fetch(source, target):
         copies.append(pltpu.make_async_copy(source, target, sems.at[len(copies)]))
         copies[-1].start()
 
-    for k in range(CHUNKS):
-        at = slice(k * width, (k + 1) * width)
+    for at in chunks:
         fetch(sketch_ref.at[at, :], table_ref.at[at, :])
         fetch(panel_ref.at[pl.ds(other, half), at], rows.at[:, at])
     fetch(panel_ref.at[pl.ds(mine, ahead_ref.shape[0]), :], ahead_ref)
-    for k in range(CHUNKS):
-        at = slice(k * width, (k + 1) * width)
+    for k, at in enumerate(chunks):
         copies[2 * k].wait()
         copies[2 * k + 1].wait()
         part = jnp.dot(rows[:, at], table_ref[at, :], preferred_element_type=F32)
@@ -110,7 +110,7 @@
         out_specs=(VMEM, VMEM, VMEM),
         scratch_shapes=[
             pltpu.VMEM((half, depth), panel.dtype),
-            pltpu.SemaphoreType.DMA((2 * CHUNKS + 1,)),
+            pltpu.SemaphoreType.DMA((2 * len(CHUNKS) + 1,)),
         ],
         cost_estimate=cost(half, depth, columns, half + ahead + columns),
         compiler_params=SMALL,
@@ -190,7 +190,8 @@
     block = 16
     for first in range(0, size, block):
         left = (size - first - block) // 8
-        look = left if left <= 4 else 3
+        lazy = left > 4
+        look = 3 if lazy else left
         count = 2 + look
         rows = [[work[first + 8 * g : first + 8 * g + 8, t] for t in tiles] for g in range(count)]
         cols = [
@@ -215,18 +216,21 @@
             units[home] = jnp.where(sublane > at, units[home], 0.0)
             for t in range(len(tiles)):
                 spread = sub(rows[home][t], at)
-                for g in range(home, count):
+                for g in range(home, 2 if lazy and t else count):
                     rows[g][t] = rows[g][t] - units[g] * spread
         for g in range(count):
             scale = lax.rsqrt(pivots[g]) if g < 2 else None
             for t, tile in enumerate(tiles):
+                if lazy and t and g >= 2:
+                    continue
                 x = rows[g][t] if scale is None else rows[g][t] * scale
                 work[first + 8 * g : first + 8 * g + 8, tile] = x
-        far = first + block + 8 * look
-        if far < size:
+        if lazy:
+            near, far = first + block, first + block + 8 * look
             done = work[first : first + block, :]
             change = dot(done[:, :HALF], done, 0, 0)
-            work[far:, :] = work[far:, :] - change[far:, :]
+            work[far:, :HALF] = work[far:, :HALF] - change[far:, :HALF]
+            work[near:, HALF:] = work[near:, HALF:] - change[near:, HALF:]
 
 
 def factor_kernel(

time: 65.3 us -> 65 us (level)
  no operation moved by 1% of the time
where the time goes in v5:
time: 65 us; the launch traced here: 64.8 us
  blocking collectives  43.9 us (68%)
  Pallas kernels  11.1 us (17%)
  starting transfers between devices  8.75 us (13%)
  between operations  0.7 us (1%)
    all_to_all x3, blocking collectives, exchanged(): return lax.all_to_all(x, axis, 0, 0, axis_index_groups=groups, tiled=True)  43.9 us
    ppermute x1, starting transfers between devices, local(): came = lax.ppermute(other, 'col', [(0, 1), (1, 0)])  8.75 us
    pallas_call x1, Pallas kernels, factor(): pl.pallas_call(functools.partial(factor_kernel, float(total_rows)), out_s...  6.03 us
    pallas_call x1, Pallas kernels, other_product(): pl.pallas_call(other_kernel, out_shape=(jax.ShapeDtypeStruct((half, colum...  2.51 us
    pallas_call x1, Pallas kernels, own_product(): pl.pallas_call(own_kernel, out_shape=jax.ShapeDtypeStruct((half, columns)...  1.93 us
  transfers between devices with their start and end apart: 1, of which 0 were waited for; matrix products, arithmetic and copies ran while one was open for 0% of the time, Pallas kernels for 3%

profile of v5, /device:TPU:1, one launch (start us, length us, event | category | flops | bytes accessed | tf_op | source)
XLA Modules:
  0.0 64.8 jit_solution(13950095228337639169)
XLA Ops:
  0.6 2.5 %other_product.1 = (f32[512,256]{1,0:T(8,128)S(1)}, bf16[2048,256]{1,0:T(8,128)(2,1)S(1)}, bf16[256,2048]{1,0:T(8,128)(2,1)S(1)}) custom-call(s32[1]{0:T(128)} %bitcast.1.core_ref, bf16[1024,2048]{1,0:T(8,128)(2,1)} %panel_ref.3, bf16[2048,256]{1,0:T(8,128)(2,1)} %sketch_ref.1), custom_call_target="tpu_custom_call" | custom-call | flops 536870912 | bytes 4718592 | tf_op jit(solution)/shard_map/other_product/pallas_call | solution.py:102
  3.1 8.7 %collective-permute-start = (f32[512,256]{1,0:T(8,128)S(1)}, f32[512,256]{1,0:T(8,128)S(1)}, u32[]{:S(2)}, u32[]{:S(2)}) collective-permute-start(f32[512,256]{1,0:T(8,128)S(1)} %get-tuple-element.9), channel_id=1, source_target_pairs={{0,1},{1,0},{2,3},{3,2},{4,5},{5,4},{6,7},{7,6},{8,9},{9,8},{10,11... | collective-permute-start | bytes 1572872 | tf_op jit(solution)/shard_map/ppermute | solution.py:339
  11.9 1.9 %own_product.1.own_ref = f32[512,256]{1,0:T(8,128)S(1)} custom-call(s32[1]{0:T(128)} %bitcast.1.core_ref, bf16[1024,2048]{1,0:T(8,128)(2,1)} %panel_ref.3, bf16[2048,256]{1,0:T(8,128)(2,1)S(1)} %get-tuple-element.7.table_ref, bf16[256,2048]{1,0:T(8,128)(2,1)S(1)} %get-tuple-element.8.ahead_ref), custom_call_target="tpu_custom_call" | custom-call | flops 536870912 | bytes 1572864 | tf_op jit(solution)/shard_map/own_product/pallas_call | solution.py:125
  13.9 0.0 collective-permute-done.came_ref
  13.9 0.6 gram.1
  14.5 10.0 %all_to_all.15 = f32[32,1,1152]{2,1,0:T(1,128)S(1)} all-to-all(f32[32,1,1152]{2,1,0:T(1,128)S(1)} %bitcast.5), channel_id=1, replica_groups=mesh['z_hi'=4,'z_lo'=2,'y_hi'=4,'y_lo'=2,'x'=4,'col'=2] {'z_lo','y_lo','..., dimensions={0} | all-to-all | bytes 294912 | tf_op jit(solution)/shard_map/all_to_all | solution.py:322
  24.5 0.1 reduce_sum.18
  24.6 21.2 %all_to_all.16 = f32[16,1,1152]{2,1,0:T(1,128)S(1)} all-to-all(f32[16,1,1152]{2,1,0:T(1,128)S(1)} %broadcast_in_dim.4), channel_id=1, replica_groups={{72,80,96,120,136,144,160,184,264,272,288,312,456,464,480,504},{64,88,1..., dimensions={0} | all-to-all | bytes 147456 | tf_op jit(solution)/shard_map/all_to_all | solution.py:322
  45.8 0.1 reduce_sum.19
  45.9 0.1 broadcast_in_dim.5
  46.0 12.8 %all_to_all.17 = f32[32,1,1152]{2,1,0:T(1,128)S(1)} all-to-all(f32[32,1,1152]{2,1,0:T(1,128)S(1)} %broadcast_in_dim.5), channel_id=1, replica_groups=mesh['z_hi'=4,'z_lo'=2,'y_hi'=4,'y_lo'=2,'x'=4,'col'=2] {'z_lo','y_lo','..., dimensions={0} | all-to-all | bytes 294912 | tf_op jit(solution)/shard_map/all_to_all | solution.py:322
  58.7 6.0 %factor.1 = (f32[512,256]{1,0:T(8,128)}, f32[256,256]{1,0:T(8,128)}) custom-call(s32[1]{0:T(128)} %bitcast.turn_ref, f32[288,128]{1,0:T(8,128)S(1)} %bitcast.4, f32[512,256]{1,0:T(8,128)S(1)} %get-tuple-element.11.block_ref), custom_call_target="tpu_custom_call" | custom-call | tf_op jit(solution)/shard_map/factor/pallas_call | solution.py:283
  (1 shorter events, 0.0 us)
Async XLA Ops:
  3.1 10.7 %collective-permute-start = (f32[512,256]{1,0:T(8,128)S(1)}, f32[512,256]{1,0:T(8,128)S(1)}, u32[]{:S(2)}, u32[]{:S(2)}) collective-permute-start(f32[512,256]{1,0:T(8,128)S(1)} %get-tuple-element.9), channel_id=1, source_target_pairs={{0,1},{1,0},{2,3},{3,2},{4,5},{5,4},{6,7},{7,6},{8,9},{9,8},{10,11... | collective-permute-start | bytes 1572872 | tf_op jit(solution)/shard_map/ppermute | solution.py:339
